TPU v7x, 32 devices: a whole 2x2x4 slice. The times are simulated.
32 devices in a mesh: frame: 8 (over z, core), head: 4 (over y, x).
Axes of the slice: x: 2, y: 2, z: 4, core: 2. Of those that a mesh axis runs over, the one named last changes fastest.
Arguments:
- queries: bfloat16 [4096, 1024], P('frame', 'head'), may hold values from -6 to 6
- key_rows: bfloat16 [4096, 1024], P('frame', 'head'), may hold values from -6 to 6
- values: bfloat16 [4096, 1024], P('frame', 'head'), may hold values from -6 to 6
- gate_init: float32 [8, 128, 128], P('head'), may hold values from -0.5 to 0.5
- up_init: float32 [8, 128, 128], P('head'), may hold values from -0.5 to 0.5
- down_init: float32 [8, 128, 128], P('head'), may hold values from -0.5 to 0.5
- step_size: float32 [8], P('head'), may hold values from 0.1 to 1
- head_scale: float32 [8], P('head'), may hold values from 0.25 to 4
- out_gain: float32 [1024], P('head'), may hold values from 0.5 to 1.5
Outputs:
- layer_out: bfloat16 [4096, 1024], P('frame', 'head')
All inputs are finite; a program needn't handle non-finite values.
Results may differ from a plain program's by a relative error of at most 0.012.
The roundings to bfloat16 on the way count: a program that leaves them out, or rounds other values in their place, can miss the bound.
Values may be sent and summed in bfloat16 or wider, within the bound.
A program may use at most 64 MiB of HBM per device.

v0:
```python
import functools
import math

import jax
import jax.numpy as jnp
from jax import lax
from jax.experimental import pallas as pl
from jax.experimental.pallas import tpu as pltpu
from jax.sharding import PartitionSpec as P

NS_ITERS = 5
GROUPS = 2
MESH = pl.DeviceIdType.MESH
SENT = jnp.bfloat16
COARSE = 2
BF = jnp.bfloat16
F32 = jnp.float32
quintic_terms = (3.4445, -4.775, 2.0315)


def dot_nt(a, b):
    return lax.dot_general(a, b, (((1,), (1,)), ((), ())), preferred_element_type=F32)


def dot_nn(a, b):
    return lax.dot_general(a, b, (((1,), (0,)), ((), ())), preferred_element_type=F32)


def dot_tn(a, b):
    return lax.dot_general(a, b, (((0,), (0,)), ((), ())), preferred_element_type=F32)


def split(x):
    high = x.astype(BF)
    return high, (x - high.astype(F32)).astype(BF)


def side(*parts):
    return jnp.concatenate(parts, axis=1)


def over(*parts):
    return jnp.concatenate(parts, axis=0)


def sigmoid(v):
    return 0.5 * (1.0 + jnp.tanh(0.5 * v))


def parts_of(x, fine):
    return split(x) if fine else (x.astype(BF),)


def left(parts):
    return side(parts[0], parts[1], parts[0]) if len(parts) == 2 else parts[0]


def right(parts, axis):
    if len(parts) == 1:
        return parts[0]
    return jnp.concatenate((parts[0], parts[0], parts[1]), axis=axis)


def newton_schulz(grads):
    xs = []
    for m in grads:
        norm = jnp.sqrt(jnp.sum(m * m, keepdims=True))
        xs.append(m * (1.0 / (norm + 1e-07)))
    for step in range(NS_ITERS):
        fine = step >= COARSE
        halves = [parts_of(x, fine) for x in xs]
        squares = [dot_nt(left(h), right(h, 1)) for h in halves]
        sq = [parts_of(a, fine) for a in squares]
        quartics = [dot_nn(left(a), right(a, 0)) for a in sq]
        mixing = [quintic_terms[1] * a + quintic_terms[2] * q for a, q in zip(squares, quartics)]
        xs = [
            quintic_terms[0] * x + dot_nn(left(parts_of(b, fine)), right(h, 0))
            for x, b, h in zip(xs, mixing, halves)
        ]
    return xs


def lengths(m, axis):
    return jnp.sqrt(jnp.sum(m * m, axis=axis, keepdims=True))


AXES = (1, 1, 0)


def kernel(
    dims,
    q_any, k_any, v_any, gate_any, up_any, down_any, gain_ref, step_ref, scale_ref,
    out_ref,
    q_ref, k_ref, v_ref, gate_ref, up_ref, down_ref, local_sem,
    kp, vp, here, before, mix, top, den, att, qn, comb, wb, wf, target, gp, rp, cs, rz, tot, fw, part, others,
    kv_send, kv_recv, pair_send, pair_recv, mate_send, mate_recv, fw_send, fw_recv,
    w_send, w_recv, head_send, head_recv,
):
    frames, nh, hd = dims
    rows, width = q_any.shape
    dh = width // hd
    half = frames // GROUPS
    mates = half // 2
    own = hd // 2
    p = lax.axis_index("frame")
    j = lax.axis_index("head")
    core = lax.rem(p, 2)
    seg = p // half
    rank = lax.rem(p, half) // 2
    pair = p + 1 - 2 * core
    has_prev = p > 0
    has_next = p < frames - 1
    prev_far = jnp.logical_and(core == 0, has_prev)
    next_far = jnp.logical_and(core == 1, has_next)

    locals_ = [
        pltpu.make_async_copy(src, dst, local_sem.at[n])
        for n, (src, dst) in enumerate(
            zip(
                (k_any, q_any, v_any, gate_any, up_any, down_any),
                (k_ref, q_ref, v_ref, gate_ref, up_ref, down_ref),
            )
        )
    ]

    def start_local():
        for copy in locals_:
            copy.start()

    def fw_targets(s):
        return [(to, r) for to in reversed(range(s + 1, GROUPS)) for r in reversed(range(mates))]

    barrier = pltpu.get_barrier_semaphore()

    def greet(frame_at, head_at):
        pl.semaphore_signal(barrier, inc=1, device_id=(frame_at, head_at), device_id_type=MESH)

    greet(pair, j)

    @pl.when(next_far)
    def _():
        greet(p + 1, j)

    @pl.when(prev_far)
    def _():
        greet(p - 1, j)

    def mate_at(step):
        return seg * half + 2 * lax.rem(rank + step, mates) + core

    def head_at(step):
        return lax.rem(j + step, nh)

    for step in range(1, mates):
        greet(mate_at(step), j)
    for step in range(1, nh):
        greet(p, head_at(step))
    is_last = rank == mates - 1
    for s in range(GROUPS):
        @pl.when(jnp.logical_and(is_last, seg == s))
        def _(s=s):
            for to, r in fw_targets(s):
                greet(to * half + 2 * r + core, j)

        @pl.when(seg > s)
        def _(s=s):
            greet(s * half + 2 * (mates - 1) + core, j)

    start_local()
    count = mates - 1 + nh - 1 + 1 + seg
    far = prev_far.astype(jnp.int32) + next_far.astype(jnp.int32)
    far = far + is_last.astype(jnp.int32) * (GROUPS - 1 - seg) * mates
    pl.semaphore_wait(barrier, count + far)

    ahead = jnp.minimum(p + 1, frames - 1)

    def kv_copy(h, which):
        src, dst = ((k_any, kp), (v_any, vp))[which]
        return pltpu.make_async_remote_copy(
            src_ref=src.at[:, pl.ds(h * dh, dh)],
            dst_ref=dst.at[h],
            send_sem=kv_send.at[2 * h + which],
            recv_sem=kv_recv.at[2 * h + which],
            device_id=(ahead, j),
            device_id_type=MESH,
        )

    @pl.when(has_next)
    def _():
        for which in range(2):
            for h in range(hd):
                kv_copy(h, which).start()

    factor = math.log2(math.e) / math.sqrt(dh)

    block = min(rows, 256)

    for copy in locals_:
        copy.wait()

    def exps(q, keys):
        scores = dot_nt(q, keys) * factor
        high = jnp.max(scores, axis=1, keepdims=True)
        e = jnp.exp2(scores - high)
        return e, high, jnp.sum(e, axis=1, keepdims=True)

    for h in range(hd):
        cols = slice(h * dh, (h + 1) * dh)
        for r in range(0, rows, block):
            rs = slice(r, r + block)
            e, t, d = exps(q_ref[rs, cols], k_ref[:, cols])
            here[h, rs] = e
            top[h, rs] = t
            den[h, rs] = d
        qf = q_ref[:, cols].astype(F32)
        mean = jnp.mean(qf * qf, axis=1, keepdims=True)
        qn[h] = (qf * lax.rsqrt(mean + 1e-06)).astype(BF)
        for m, ref in enumerate((gate_ref, up_ref, down_ref)):
            w = ref[h]
            w = w.T if AXES[m] else w
            high, low = split(w)
            wb[0, h, m] = side(high, low)
    for i in range(own):
        h = core * own + i
        for m, ref in enumerate((gate_ref, up_ref, down_ref)):
            w = ref[h]
            w = w.T if AXES[m] else w
            wf[i, m] = w
            target[i, m] = jnp.broadcast_to(lengths(w, AXES[m]), w.shape)

    @pl.when(has_prev)
    def _():
        for h in range(hd):
            cols = slice(h * dh, (h + 1) * dh)
            kv_copy(h, 0).wait_recv()
            for r in range(0, rows, block):
                rs = slice(r, r + block)
                e, t, d = exps(q_ref[rs, cols], kp[h])
                t0 = top[h, rs]
                high = jnp.maximum(t, t0)
                a, b = jnp.exp2(t0 - high), jnp.exp2(t - high)
                inv = 1.0 / (den[h, rs] * a + d * b)
                before[h, rs] = (e * (b * inv)).astype(BF)
                probs = (here[h, rs] * (a * inv)).astype(BF)
                mix[h, rs] = dot_nn(probs, v_ref[:, cols])

    @pl.when(jnp.logical_not(has_prev))
    def _():
        for h in range(hd):
            cols = slice(h * dh, (h + 1) * dh)
            for r in range(0, rows, block):
                rs = slice(r, r + block)
                probs = (here[h, rs] * (1.0 / den[h, rs])).astype(BF)
                mix[h, rs] = dot_nn(probs, v_ref[:, cols])

    for h in range(hd):
        @pl.when(has_prev)
        def _(h=h):
            kv_copy(h, 1).wait_recv()
            mix[h] = mix[h] + dot_nn(before[h], vp[h])

        m = mix[h]
        mean = jnp.mean(m * m, axis=1, keepdims=True)
        att[h] = (m * lax.rsqrt(mean + 1e-06)).astype(BF)

    def pair_copy(i, m):
        return pltpu.make_async_remote_copy(
            src_ref=gp.at[(1 - core) * own + i, m],
            dst_ref=rp.at[i, m],
            send_sem=pair_send.at[i * 3 + m],
            recv_sem=pair_recv.at[i * 3 + m],
            device_id=(pair, j),
            device_id_type=MESH,
        )

    def mate_copy(step, i, m):
        return pltpu.make_async_remote_copy(
            src_ref=cs.at[i, m],
            dst_ref=rz.at[step - 1, i, m],
            send_sem=mate_send.at[step - 1, i * 3 + m],
            recv_sem=mate_recv.at[step - 1, i * 3 + m],
            device_id=(mate_at(step), j),
            device_id_type=MESH,
        )

    def fw_copy(s, to, r, i, m):
        return pltpu.make_async_remote_copy(
            src_ref=cs.at[own + i, m],
            dst_ref=fw.at[s, i, m],
            send_sem=fw_send.at[(to - s - 1) * mates + r, i * 3 + m],
            recv_sem=fw_recv.at[s, i * 3 + m],
            device_id=(to * half + 2 * r + core, j),
            device_id_type=MESH,
        )

    def w_copy(state, i, m, which):
        at = which * own + i
        span = pl.ds(0, dh if state == GROUPS else 2 * dh)
        return pltpu.make_async_remote_copy(
            src_ref=wb.at[state, at, m, :, span],
            dst_ref=wb.at[state, at, m, :, span],
            send_sem=w_send.at[state - 1, i * 3 + m],
            recv_sem=w_recv.at[state - 1, i * 3 + m],
            device_id=(pair, j),
            device_id_type=MESH,
        )

    def fast_grads(state, h):
        x = att[h]
        y = v_ref[:, pl.ds(pl.multiple_of(h * dh, dh), dh)]
        xx = side(x, x)
        gate = dot_nt(wb[state, h, 0], xx)
        upward = dot_nt(wb[state, h, 1], xx)
        back = -dot_nt(wb[state, h, 2], side(y, y))
        sig = sigmoid(gate)
        active = gate * sig
        hidden = active * upward
        gp[h, 2] = -dot_nn(hidden.astype(BF), y)
        back_gate = back * upward * sig * (1.0 + gate * (1.0 - sig))
        gp[h, 0] = dot_nn(back_gate.astype(BF), x)
        gp[h, 1] = dot_nn((back * active).astype(BF), x)

    for s in range(GROUPS):
        @pl.when(seg == s)
        def _(s=s):
            for i in range(own):
                fast_grads(s, (1 - core) * own + i)
                for m in range(3):
                    pair_copy(i, m).start()
            for i in range(own):
                fast_grads(s, core * own + i)
            for i in range(own):
                for m in range(3):
                    pair_copy(i, m).wait_recv()
                    chip = gp[core * own + i, m] + rp[i, m]
                    cs[i, m] = chip.astype(SENT)
                    for step in range(1, mates):
                        mate_copy(step, i, m).start()
                    tot[i, m] = chip
            for i in range(own):
                for m in range(3):
                    total = tot[i, m]
                    for step in range(1, mates):
                        mate_copy(step, i, m).wait_recv()
                        total = total + rz[step - 1, i, m].astype(F32)
                    tot[i, m] = total
                    if s < GROUPS - 1:
                        cs[own + i, m] = total.astype(SENT)

                        @pl.when(rank == mates - 1)
                        def _(i=i, m=m):
                            fw_copy(s, *fw_targets(s)[0], i, m).start()

            if s < GROUPS - 1:
                @pl.when(rank == mates - 1)
                def _():
                    for to, r in fw_targets(s)[1:]:
                        for i in range(own):
                            for m in range(3):
                                fw_copy(s, to, r, i, m).start()

        if s < GROUPS - 1:
            @pl.when(seg > s)
            def _(s=s):
                for i in range(own):
                    for m in range(3):
                        fw_copy(s, s + 1, 0, i, m).wait_recv()
                        tot[i, m] = fw[s, i, m].astype(F32)

        @pl.when(seg >= s)
        def _(s=s):
            for i in range(own):
                at = core * own + i
                rate = step_ref[at]
                ortho = newton_schulz([tot[i, m] for m in range(3)])
                for m in range(3):
                    moved = wf[i, m] - rate * ortho[m]
                    w = moved * (target[i, m] / (lengths(moved, AXES[m]) + 1e-06))
                    if s < GROUPS - 1:
                        wf[i, m] = w
                    high, low = split(w)
                    wb[s + 1, at, m] = side(high, low)
                    w_copy(s + 1, i, m, core).start()
            for i in range(own):
                for m in range(3):
                    w_copy(s + 1, i, m, 1 - core).wait_recv()

    ones = jnp.ones((8, dh), BF)
    sums = jnp.zeros((8, rows), F32)
    mine = seg + 1
    for h in range(hd):
        cols = slice(h * dh, (h + 1) * dh)
        x = qn[h]
        gate = dot_nt(x, wb[mine, h, 0][:, :dh])
        upward = dot_nt(x, wb[mine, h, 1][:, :dh])
        hidden = (gate * sigmoid(gate) * upward).astype(BF)
        out = dot_nn(hidden, wb[mine, h, 2][:, :dh])
        fast = (out * scale_ref[h]).astype(BF)
        both = att[h].astype(F32) + fast.astype(F32)
        comb[:, cols] = both
        high, low = split(both * both)
        sums = sums + dot_nt(side(ones, ones), side(high, low))
    sums = jnp.maximum(sums, 0.0)
    part[...] = sums

    def head_copy(step):
        return pltpu.make_async_remote_copy(
            src_ref=part,
            dst_ref=others.at[step - 1],
            send_sem=head_send.at[step - 1],
            recv_sem=head_recv.at[step - 1],
            device_id=(p, head_at(step)),
            device_id_type=MESH,
        )

    for step in range(1, nh):
        head_copy(step).start()
    for step in range(1, nh):
        head_copy(step).wait_recv()
        sums = sums + others[step - 1]
    high, low = split(lax.rsqrt(sums / (width * nh) + 1e-05))
    eighths = jnp.full((16, dh), 0.125, BF)
    inverse = dot_tn(over(high.astype(F32), low.astype(F32)).astype(BF), eighths)
    for h in range(hd):
        cols = slice(h * dh, (h + 1) * dh)
        out_ref[:, cols] = comb[:, cols] * inverse

    for step in range(1, nh):
        head_copy(step).wait_send()

    @pl.when(has_next)
    def _():
        for h in range(hd):
            for which in range(2):
                kv_copy(h, which).wait_send()

    for i in range(own):
        for m in range(3):
            pair_copy(i, m).wait_send()
            for step in range(1, mates):
                mate_copy(step, i, m).wait_send()
    for s in range(GROUPS):
        @pl.when(seg >= s)
        def _(s=s):
            for i in range(own):
                for m in range(3):
                    w_copy(s + 1, i, m, core).wait_send()

        if s < GROUPS - 1:
            @pl.when(jnp.logical_and(seg == s, rank == mates - 1))
            def _(s=s):
                for to, r in fw_targets(s):
                    for i in range(own):
                        for m in range(3):
                            fw_copy(s, to, r, i, m).wait_send()


def shards(
    queries, key_rows, values, gate_init, up_init, down_init, step_size, head_scale, out_gain
):
    rows, width = queries.shape
    hd, dh, fwh = gate_init.shape
    frames, nh = lax.axis_size("frame"), lax.axis_size("head")
    mates = frames // GROUPS // 2
    own = hd // 2
    dma = pltpu.SemaphoreType.DMA
    vmem = pl.BlockSpec(memory_space=pltpu.VMEM)
    smem = pl.BlockSpec(memory_space=pltpu.SMEM)
    scaled = pl.pallas_call(
        functools.partial(kernel, (frames, nh, hd)),
        out_shape=jax.ShapeDtypeStruct((rows, width), F32),
        in_specs=[pl.BlockSpec(memory_space=pl.ANY)] * 6 + [vmem] + [smem] * 2,
        out_specs=vmem,
        scratch_shapes=[
            pltpu.VMEM((rows, width), BF),
            pltpu.VMEM((rows, width), BF),
            pltpu.VMEM((rows, width), BF),
            pltpu.VMEM((hd, dh, fwh), F32),
            pltpu.VMEM((hd, dh, fwh), F32),
            pltpu.VMEM((hd, fwh, dh), F32),
            dma((6,)),
            pltpu.VMEM((hd, rows, dh), BF),
            pltpu.VMEM((hd, rows, dh), BF),
            pltpu.VMEM((hd, rows, rows), F32),
            pltpu.VMEM((hd, rows, rows), BF),
            pltpu.VMEM((hd, rows, dh), F32),
            pltpu.VMEM((hd, rows, 1), F32),
            pltpu.VMEM((hd, rows, 1), F32),
            pltpu.VMEM((hd, rows, dh), BF),
            pltpu.VMEM((hd, rows, dh), BF),
            pltpu.VMEM((rows, width), F32),
            pltpu.VMEM((GROUPS + 1, hd, 3, dh, 2 * fwh), BF),
            pltpu.VMEM((own, 3, dh, fwh), F32),
            pltpu.VMEM((own, 3, dh, fwh), F32),
            pltpu.VMEM((hd, 3, dh, fwh), F32),
            pltpu.VMEM((own, 3, dh, fwh), F32),
            pltpu.VMEM((2 * own, 3, dh, fwh), SENT),
            pltpu.VMEM((max(mates - 1, 1), own, 3, dh, fwh), SENT),
            pltpu.VMEM((own, 3, dh, fwh), F32),
            pltpu.VMEM((GROUPS - 1, own, 3, dh, fwh), SENT),
            pltpu.VMEM((8, rows), F32),
            pltpu.VMEM((max(nh - 1, 1), 8, rows), F32),
            dma((2 * hd,)), dma((2 * hd,)),
            dma((own * 3,)), dma((own * 3,)),
            dma((max(mates - 1, 1), own * 3)), dma((max(mates - 1, 1), own * 3)),
            dma(((GROUPS - 1) * mates, own * 3)), dma((GROUPS - 1, own * 3)),
            dma((GROUPS, own * 3)), dma((GROUPS, own * 3)),
            dma((max(nh - 1, 1),)), dma((max(nh - 1, 1),)),
        ],
        compiler_params=pltpu.CompilerParams(
            collective_id=0, has_side_effects=True, vmem_limit_bytes=56 * 1024 * 1024
        ),
    )(
        queries, key_rows, values, gate_init, up_init, down_init,
        out_gain.reshape(1, width), step_size, head_scale,
    )
    return (scaled * out_gain[None, :]).astype(BF)


def solution(mesh):
    in_specs = (
        P("frame", "head"),
        P("frame", "head"),
        P("frame", "head"),
        P("head", None, None),
        P("head", None, None),
        P("head", None, None),
        P("head"),
        P("head"),
        P("head"),
    )
    return jax.shard_map(
        shards, mesh=mesh, in_specs=in_specs, out_specs=P("frame", "head"), check_vma=False
    )
```

profile of v0, /device:TPU:25, one launch (start us, length us, event | category | flops | bytes accessed | tf_op | source)
XLA Modules:
  0.0 37.9 jit_solution(11312339406754355489)
XLA Ops:
  0.0 0.0 copy-start
  0.0 36.1 %shard_map.91 = f32[512,256]{1,0:T(8,128)} custom-call(bf16[512,256]{1,0:T(8,128)(2,1)} %q_any.1, bf16[512,256]{1,0:T(8,128)(2,1)} %k_any.1, bf16[512,256]{1,0:T(8,128)(2,1)} %v_any.1, f32[2,128,128]{2,1,0:T(8,128)} %gate_any.1, f32[2,128,128]{2,1,0:T(8,128)} %up_any.1, f32[2,128,128]{2,1,0:T(8,128)} %down_any.1, f32[1,256]{1,0:T(1,128)} %bitcast.1, ...), custom_call_target="tpu_custom_call" | custom-call | tf_op jit(solution)/shard_map/pallas_call | solution.py:469
  36.1 0.0 copy-done
  36.1 1.8 %multiply_convert_fusion = bf16[512,256]{1,0:T(8,128)(2,1)} fusion(f32[512,256]{1,0:T(8,128)} %shard_map.91, f32[256]{0:T(256)S(1)} %copy-done), kind=kLoop, calls=%fused_computation | loop fusion | flops 262144 | bytes 787456 | tf_op jit(solution)/shard_map/convert_element_type | solution.py:517
Async XLA Ops:
  0.0 36.1 %copy-start = (f32[256]{0:T(256)S(1)}, f32[256]{0:T(256)}, u32[]{:S(2)}) copy-start(f32[256]{0:T(256)} %param.17) | copy-start | bytes 3076
where the time goes:
time: 38.1 us; the launch traced here: 37.9 us
  Pallas kernels  36.1 us (95%)
  other arithmetic  1.78 us (5%)
    pallas_call x1, Pallas kernels, shards(): pl.pallas_call(functools.partial(kernel, (frames, nh, hd)), out_shape=jax...  36.1 us
    convert_element_type x1, other arithmetic, shards(): return (scaled * out_gain[None, :]).astype(BF)  1.78 us

commit v1 on v0

v1 whole, which is shorter than its diff:
```python
import functools
import math

import jax
import jax.numpy as jnp
from jax import lax
from jax.experimental import pallas as pl
from jax.experimental.pallas import tpu as pltpu
from jax.sharding import PartitionSpec as P

NS_ITERS = 5
GROUPS = 2
MESH = pl.DeviceIdType.MESH
SENT = jnp.bfloat16
COARSE = 2
BF = jnp.bfloat16
F32 = jnp.float32
quintic_terms = (3.4445, -4.775, 2.0315)


def dot_nt(a, b):
    return lax.dot_general(a, b, (((1,), (1,)), ((), ())), preferred_element_type=F32)


def dot_nn(a, b):
    return lax.dot_general(a, b, (((1,), (0,)), ((), ())), preferred_element_type=F32)


def dot_tn(a, b):
    return lax.dot_general(a, b, (((0,), (0,)), ((), ())), preferred_element_type=F32)


def split(x):
    high = x.astype(BF)
    return high, (x - high.astype(F32)).astype(BF)


def side(*parts):
    return jnp.concatenate(parts, axis=1)


def over(*parts):
    return jnp.concatenate(parts, axis=0)


def sigmoid(v):
    return 0.5 * (1.0 + jnp.tanh(0.5 * v))


def parts_of(x, fine):
    return split(x) if fine else (x.astype(BF),)


def left(parts):
    return side(parts[0], parts[1], parts[0]) if len(parts) == 2 else parts[0]


def right(parts, axis):
    if len(parts) == 1:
        return parts[0]
    return jnp.concatenate((parts[0], parts[0], parts[1]), axis=axis)


def newton_schulz(grads):
    xs = []
    for m in grads:
        norm = jnp.sqrt(jnp.sum(m * m, keepdims=True))
        xs.append(m * (1.0 / (norm + 1e-07)))
    for step in range(NS_ITERS):
        fine = step >= COARSE
        halves = [parts_of(x, fine) for x in xs]
        squares = [dot_nt(left(h), right(h, 1)) for h in halves]
        sq = [parts_of(a, fine) for a in squares]
        quartics = [dot_nn(left(a), right(a, 0)) for a in sq]
        mixing = [quintic_terms[1] * a + quintic_terms[2] * q for a, q in zip(squares, quartics)]
        xs = [
            quintic_terms[0] * x + dot_nn(left(parts_of(b, fine)), right(h, 0))
            for x, b, h in zip(xs, mixing, halves)
        ]
    return xs


def lengths(m, axis):
    return jnp.sqrt(jnp.sum(m * m, axis=axis, keepdims=True))


AXES = (1, 1, 0)
ORDER = (2, 0, 1)


def kernel(
    dims,
    q_any, k_any, v_any, gate_any, up_any, down_any, step_any, scale_any,
    out_ref,
    qs, ks, vs, gate_ref, up_ref, down_ref, step_ref, scale_ref, local_sem,
    kp, here, before, mix, top, den, att, qn, comb, wb, wf, target, gp, hid, backs, cs, rz, tot, fw, by, wo, wr, part, others, frame_sem, head_sem, by_send, by_recv,
    kv_send, kv_recv, y_send, y_recv, att_send, att_recv, mate_send, mate_recv, fw_send, fw_recv,
    w_send, w_recv, head_send, head_recv,
):
    frames, nh, hd = dims
    rows, width = q_any.shape
    dh = width // hd
    half = frames // GROUPS
    mates = half // 2
    own = hd // 2
    p = lax.axis_index("frame")
    j = lax.axis_index("head")
    core = lax.rem(p, 2)
    seg = p // half
    rank = lax.rem(p, half) // 2
    pair = p + 1 - 2 * core
    has_prev = p > 0
    has_next = p < frames - 1
    prev_far = jnp.logical_and(core == 0, has_prev)
    next_far = jnp.logical_and(core == 1, has_next)

    def head_of(n, c):
        return (1 - c) * own + n if n < own else c * own + n - own

    def cols_of(h):
        return pl.ds(pl.multiple_of(h * dh, dh), dh)

    mine = pl.ds(core * own, own)
    moves = []
    for n in range(hd):
        cols = cols_of(head_of(n, core))
        for src, dst in ((k_any, ks), (q_any, qs), (v_any, vs)):
            moves.append((src.at[:, cols], dst.at[n]))
    moves += [
        (gate_any.at[mine], gate_ref), (up_any.at[mine], up_ref), (down_any.at[mine], down_ref),
        (step_any, step_ref), (scale_any, scale_ref),
    ]
    locals_ = [pltpu.make_async_copy(src, dst, local_sem.at[n]) for n, (src, dst) in enumerate(moves)]

    barrier = pltpu.get_barrier_semaphore()

    def signal(sem, frame_at, head_at):
        pl.semaphore_signal(sem, inc=1, device_id=(frame_at, head_at), device_id_type=MESH)

    def mate_at(step):
        return seg * half + 2 * lax.rem(rank + step, mates) + core

    def head_at(step):
        return lax.rem(j + step, nh)

    def flip(bit):
        return j + bit - 2 * bit * lax.rem(j // bit, 2)

    is_last = rank == mates - 1
    paired = nh & (nh - 1) == 0
    bits = [1 << k for k in range(nh.bit_length() - 1)]
    partners = [flip(bit) for bit in bits] if paired else [head_at(step) for step in range(1, nh)]

    def ring_signal(sem, reach):
        @pl.when(p + reach < frames)
        def _():
            signal(sem, p + reach, j)

        @pl.when(p >= reach)
        def _():
            signal(sem, p - reach, j)

    def ring_count(reach):
        return (p + reach < frames).astype(jnp.int32) + (p >= reach).astype(jnp.int32)

    signal(barrier, pair, j)

    @pl.when(next_far)
    def _():
        signal(barrier, p + 1, j)

    @pl.when(prev_far)
    def _():
        signal(barrier, p - 1, j)

    ring_signal(barrier, 2)
    for to in partners:
        signal(barrier, p, to)
    for copy in locals_:
        copy.start()
    far = prev_far.astype(jnp.int32) + next_far.astype(jnp.int32)
    pl.semaphore_wait(barrier, 1 + far + ring_count(2) + len(partners))

    frame_rounds = max((mates - 1).bit_length(), 0)
    head_rounds = len(bits) - 1 if paired else 0

    def frame_signal(k):
        ring_signal(frame_sem.at[k], 2 << k)

    def head_signal(k):
        for to in partners:
            signal(head_sem.at[k], p, to)

    def rounds():
        for k in range(frame_rounds):
            pl.semaphore_wait(frame_sem.at[k], ring_count(2 << k))
            if k + 1 < frame_rounds:
                frame_signal(k + 1)
        for k in range(head_rounds):
            pl.semaphore_wait(head_sem.at[k], len(partners))
            if k + 1 < head_rounds:
                head_signal(k + 1)

    ahead = jnp.minimum(p + 1, frames - 1)

    def kv_copy(n, which):
        cols = cols_of(head_of(n, 1 - core))
        src, dst = ((k_any, kp.at[n]), (v_any, vs.at[hd + n]))[which]
        return pltpu.make_async_remote_copy(
            src_ref=src.at[:, cols],
            dst_ref=dst,
            send_sem=kv_send.at[2 * n + which],
            recv_sem=kv_recv.at[2 * n + which],
            device_id=(ahead, j),
            device_id_type=MESH,
        )

    def y_copy(i):
        return pltpu.make_async_remote_copy(
            src_ref=v_any.at[:, pl.ds(i * dh, dh)],
            dst_ref=vs.at[2 * hd + i],
            send_sem=y_send.at[i],
            recv_sem=y_recv.at[i],
            device_id=(pair, j),
            device_id_type=MESH,
        )

    def att_copy(i):
        return pltpu.make_async_remote_copy(
            src_ref=att.at[i],
            dst_ref=att.at[hd + i],
            send_sem=att_send.at[i],
            recv_sem=att_recv.at[i],
            device_id=(pair, j),
            device_id_type=MESH,
        )

    @pl.when(has_next)
    def _():
        for n in range(hd):
            for which in range(2):
                kv_copy(n, which).start()

    @pl.when(core == 1)
    def _():
        for i in range(own):
            y_copy(i).start()

    if frame_rounds:
        frame_signal(0)
    if head_rounds:
        head_signal(0)

    factor = math.log2(math.e) / math.sqrt(dh)

    block = min(rows, 256)

    for copy in locals_:
        copy.wait()

    def exps(q, keys):
        scores = dot_nt(q, keys) * factor
        high = jnp.max(scores, axis=1, keepdims=True)
        e = jnp.exp2(scores - high)
        return e, high, jnp.sum(e, axis=1, keepdims=True)

    for n in range(hd):
        for r in range(0, rows, block):
            rs = slice(r, r + block)
            e, t, d = exps(qs[n, rs], ks[n])
            here[n, rs] = e
            top[n, rs] = t
            den[n, rs] = d
        qf = qs[n].astype(F32)
        mean = jnp.mean(qf * qf, axis=1, keepdims=True)
        qn[n] = (qf * lax.rsqrt(mean + 1e-06)).astype(BF)
    for i in range(own):
        for m, ref in enumerate((gate_ref, up_ref, down_ref)):
            w = ref[i]
            w = w.T if AXES[m] else w
            wf[i, m] = w
            target[i, m] = jnp.broadcast_to(lengths(w, AXES[m]), w.shape)
            high, low = split(w)
            wb[0, i, m] = side(high, low)

    def weigh(n):
        @pl.when(has_prev)
        def _():
            kv_copy(n, 0).wait_recv()
            for r in range(0, rows, block):
                rs = slice(r, r + block)
                e, t, d = exps(qs[n, rs], kp[n])
                t0 = top[n, rs]
                high = jnp.maximum(t, t0)
                a, b = jnp.exp2(t0 - high), jnp.exp2(t - high)
                inv = 1.0 / (den[n, rs] * a + d * b)
                before[n, rs] = (e * (b * inv)).astype(BF)
                probs = (here[n, rs] * (a * inv)).astype(BF)
                mix[n, rs] = dot_nn(probs, vs[n])

        @pl.when(jnp.logical_not(has_prev))
        def _():
            for r in range(0, rows, block):
                rs = slice(r, r + block)
                probs = (here[n, rs] * (1.0 / den[n, rs])).astype(BF)
                mix[n, rs] = dot_nn(probs, vs[n])

    def attend(n):
        @pl.when(has_prev)
        def _():
            kv_copy(n, 1).wait_recv()
            mix[n] = mix[n] + dot_nn(before[n], vs[hd + n])

        m = mix[n]
        mean = jnp.mean(m * m, axis=1, keepdims=True)
        att[n] = (m * lax.rsqrt(mean + 1e-06)).astype(BF)

    for n in range(own):
        weigh(n)
        attend(n)
        att_copy(n).start()
    rounds()

    def mate_copy(step, i, m):
        return pltpu.make_async_remote_copy(
            src_ref=cs.at[i, m],
            dst_ref=rz.at[step - 1, i, m],
            send_sem=mate_send.at[step - 1, i * 3 + m],
            recv_sem=mate_recv.at[step - 1, i * 3 + m],
            device_id=(mate_at(step), j),
            device_id_type=MESH,
        )

    beyond = jnp.minimum(p + 2, frames - 1)

    def fw_copy(src, frame_at, k, i, m):
        return pltpu.make_async_remote_copy(
            src_ref=src,
            dst_ref=fw.at[i, m],
            send_sem=fw_send.at[k, i * 3 + m],
            recv_sem=fw_recv.at[i * 3 + m],
            device_id=(frame_at, j),
            device_id_type=MESH,
        )

    def fw_direct(k, i, m):
        return fw_copy(cs.at[own + i, m], half + 2 * k + core, k, i, m)

    def relay(i, m):
        return fw_copy(fw.at[i, m], beyond, 0, i, m)

    def aside(i, m):
        return pltpu.make_async_remote_copy(
            src_ref=cs.at[own + i, m],
            dst_ref=by.at[i, m],
            send_sem=by_send.at[i * 3 + m],
            recv_sem=by_recv.at[i * 3 + m],
            device_id=(pair, j),
            device_id_type=MESH,
        )

    def behalf(i, m):
        return fw_copy(by.at[i, m], ahead, mates, i, m)

    def fw_sends(c, i, m):
        if m == ORDER[-1]:
            return [fw_direct(k, i, m) for k in reversed(range(mates))]
        if c == 1:
            return [fw_direct(0, i, m)]
        return [fw_direct(k, i, m) for k in reversed(range(1, mates))] + [aside(i, m)]

    relays = jnp.logical_and(core == 1, p < frames - 2)
    closes = jnp.logical_and(seg == 0, is_last)

    def w_copy(i, m):
        return pltpu.make_async_remote_copy(
            src_ref=wo.at[i, m],
            dst_ref=wr.at[i, m],
            send_sem=w_send.at[i * 3 + m],
            recv_sem=w_recv.at[i * 3 + m],
            device_id=(pair, j),
            device_id_type=MESH,
        )

    always = p < frames

    def fast_grads(state, i, sets, finish):
        @pl.when(always)
        def _():
            total = None
            for k, (xi, yi) in enumerate(sets):
                x = att[xi]
                xx = side(x, x)
                gate = dot_nt(wb[state, i, 0], xx)
                upward = dot_nt(wb[state, i, 1], xx)
                sig = sigmoid(gate)
                active = gate * sig
                hid[k, 0] = active
                hid[k, 1] = upward * sig * (1.0 + gate * (1.0 - sig))
                d = dot_nn((active * upward).astype(BF), vs[yi])
                total = d if total is None else total + d
            finish(i, 2, -total)

        @pl.when(always)
        def _():
            total = None
            for k, (xi, yi) in enumerate(sets):
                y = vs[yi]
                back = -dot_nt(wb[state, i, 2], side(y, y))
                backs[k] = (back * hid[k, 0]).astype(BF)
                d = dot_nn((back * hid[k, 1]).astype(BF), att[xi])
                total = d if total is None else total + d
            finish(i, 0, total)

        @pl.when(always)
        def _():
            total = None
            for k, (xi, yi) in enumerate(sets):
                d = dot_nn(backs[k], att[xi])
                total = d if total is None else total + d
            finish(i, 1, total)

    def keep(i, m, value):
        gp[i, m] = value

    def mate_start(i, m):
        for step in range(1, mates):
            mate_copy(step, i, m).start()

    def with_mates(i, m, total):
        for step in range(1, mates):
            mate_copy(step, i, m).wait_recv()
            total = total + rz[step - 1, i, m].astype(F32)
        return total

    def share(i, m, value):
        tot[i, m] = value
        cs[i, m] = value.astype(SENT)
        mate_start(i, m)

    def share_late(i, m, value):
        value = value + gp[i, m]
        cs[i, m] = value.astype(SENT)
        tot[i, m] = value

        @pl.when(jnp.logical_not(is_last))
        def _():
            mate_start(i, m)

        @pl.when(is_last)
        def _():
            total = with_mates(i, m, tot[i, m])
            tot[i, m] = total
            cs[own + i, m] = total.astype(SENT)

        for c in range(2):
            @pl.when(jnp.logical_and(is_last, core == c))
            def _(c=c):
                for copy in fw_sends(c, i, m):
                    copy.start()

    def pair_wait(i):
        att_copy(i).wait_recv()

        @pl.when(core == 0)
        def _():
            y_copy(i).wait_recv()

    hold = prev_far.astype(jnp.int32)

    def pair_set(i):
        return hd + i, 2 * hd + i - core * (hd - own)

    def early_set(i):
        return own + i + hold * (hd - own), own + i + hold * (2 * hd - own)

    def late_set(i):
        x, y = pair_set(i)
        return x + hold * (own + i - x), y + hold * (own + i - y)

    opening = seg == 0
    first_pair = jnp.logical_and(opening, prev_far)

    @pl.when(first_pair)
    def _():
        for i in range(own):
            pair_wait(i)
            fast_grads(0, i, [early_set(i)], keep)

    for n in range(own, hd):
        weigh(n)
        attend(n)

    @pl.when(jnp.logical_and(opening, jnp.logical_not(prev_far)))
    def _():
        for i in range(own):
            fast_grads(0, i, [early_set(i)], keep)
            pair_wait(i)

    for s in range(GROUPS):
        @pl.when(seg == s)
        def _(s=s):
            for i in range(own):
                if s == 0:
                    fast_grads(s, i, [late_set(i)], share_late)
                else:
                    pair_wait(i)
                    fast_grads(s, i, [(own + i, own + i), pair_set(i)], share)
            if s == 0:
                @pl.when(jnp.logical_and(is_last, core == 1))
                def _():
                    for m in ORDER[:-1]:
                        for i in range(own):
                            aside(i, m).wait_recv()
                            behalf(i, m).start()

                @pl.when(is_last)
                def _():
                    for m in ORDER:
                        for i in range(own):
                            mate_start(i, m)

                @pl.when(jnp.logical_not(is_last))
                def _():
                    for m in ORDER:
                        for i in range(own):
                            tot[i, m] = with_mates(i, m, tot[i, m])
            else:
                for m in ORDER:
                    for i in range(own):
                        tot[i, m] = with_mates(i, m, tot[i, m])

        if s == 0:
            @pl.when(seg > 0)
            def _():
                for m in ORDER:
                    for i in range(own):
                        relay(i, m).wait_recv()
                        if m != ORDER[-1]:
                            @pl.when(relays)
                            def _(i=i, m=m):
                                relay(i, m).start()

                        tot[i, m] = fw[i, m].astype(F32)

        @pl.when(seg >= s)
        def _(s=s):
            for i in range(own):
                rate = step_ref[core * own + i]
                ortho = newton_schulz([tot[i, m] for m in range(3)])
                for m in range(3):
                    moved = wf[i, m] - rate * ortho[m]
                    w = moved * (target[i, m] / (lengths(moved, AXES[m]) + 1e-06))
                    high, low = split(w)
                    wo[i, m] = high
                    if s < GROUPS - 1:
                        wf[i, m] = w
                        wb[s + 1, i, m] = side(high, low)

            @pl.when(seg == s)
            def _():
                for i in range(own):
                    for m in range(3):
                        w_copy(i, m).start()

    ones = jnp.ones((8, dh), BF)
    sums = jnp.zeros((8, rows), F32)
    for n in [*range(own, hd), *range(own)]:
        if n < own:
            for m in range(3):
                w_copy(n, m).wait_recv()
        final = wr if n < own else wo
        i = n if n < own else n - own
        x = qn[n]
        gate = dot_nt(x, final[i, 0])
        upward = dot_nt(x, final[i, 1])
        hidden = (gate * sigmoid(gate) * upward).astype(BF)
        out = dot_nn(hidden, final[i, 2])
        fast = (out * scale_ref[head_of(n, core)]).astype(BF)
        both = att[n].astype(F32) + fast.astype(F32)
        comb[n] = both
        high, low = split(both * both)
        sums = sums + dot_nt(side(ones, ones), side(high, low))
    sums = jnp.maximum(sums, 0.0)
    part[...] = sums[:1]

    def head_copy(step):
        return pltpu.make_async_remote_copy(
            src_ref=part,
            dst_ref=others.at[step - 1],
            send_sem=head_send.at[step - 1],
            recv_sem=head_recv.at[step - 1],
            device_id=(p, head_at(step)),
            device_id_type=MESH,
        )

    for step in range(1, nh):
        head_copy(step).start()
    total = sums[:1]
    for step in range(1, nh):
        head_copy(step).wait_recv()
        total = total + others[step - 1]
    total = jnp.broadcast_to(total, (8, rows))
    high, low = split(lax.rsqrt(total / (width * nh) + 1e-05))
    eighths = jnp.full((16, dh), 0.125, BF)
    inverse = dot_tn(over(high.astype(F32), low.astype(F32)).astype(BF), eighths)
    for n in range(hd):
        out_ref[:, cols_of(head_of(n, core))] = comb[n] * inverse

    for step in range(1, nh):
        head_copy(step).wait_send()

    @pl.when(has_next)
    def _():
        for n in range(hd):
            for which in range(2):
                kv_copy(n, which).wait_send()

    @pl.when(core == 1)
    def _():
        for i in range(own):
            y_copy(i).wait_send()

    for i in range(own):
        att_copy(i).wait_send()
        for m in range(3):
            w_copy(i, m).wait_send()
            for step in range(1, mates):
                mate_copy(step, i, m).wait_send()
    for c in range(2):
        @pl.when(jnp.logical_and(closes, core == c))
        def _(c=c):
            for i in range(own):
                for m in range(3):
                    for copy in fw_sends(c, i, m):
                        copy.wait_send()
                    if c == 1 and m != ORDER[-1]:
                        behalf(i, m).wait_send()

    @pl.when(jnp.logical_and(seg > 0, relays))
    def _():
        for i in range(own):
            for m in ORDER[:-1]:
                relay(i, m).wait_send()


def shards(
    queries, key_rows, values, gate_init, up_init, down_init, step_size, head_scale, out_gain
):
    rows, width = queries.shape
    hd, dh, fwh = gate_init.shape
    frames, nh = lax.axis_size("frame"), lax.axis_size("head")
    mates = frames // GROUPS // 2
    own = hd // 2
    dma = pltpu.SemaphoreType.DMA
    vmem = pl.BlockSpec(memory_space=pltpu.VMEM)
    scaled = pl.pallas_call(
        functools.partial(kernel, (frames, nh, hd)),
        out_shape=pltpu.VMEM((rows, width), F32),
        in_specs=[pl.BlockSpec(memory_space=pl.ANY)] * 8,
        out_specs=vmem,
        scratch_shapes=[
            pltpu.VMEM((hd, rows, dh), BF),
            pltpu.VMEM((hd, rows, dh), BF),
            pltpu.VMEM((2 * hd + own, rows, dh), BF),
            pltpu.VMEM((own, dh, fwh), F32),
            pltpu.VMEM((own, dh, fwh), F32),
            pltpu.VMEM((own, fwh, dh), F32),
            pltpu.SMEM((hd,), F32),
            pltpu.SMEM((hd,), F32),
            dma((3 * hd + 5,)),
            pltpu.VMEM((hd, rows, dh), BF),
            pltpu.VMEM((hd, rows, rows), F32),
            pltpu.VMEM((hd, rows, rows), BF),
            pltpu.VMEM((hd, rows, dh), F32),
            pltpu.VMEM((hd, rows, 1), F32),
            pltpu.VMEM((hd, rows, 1), F32),
            pltpu.VMEM((hd + own, rows, dh), BF),
            pltpu.VMEM((hd, rows, dh), BF),
            pltpu.VMEM((hd, rows, dh), F32),
            pltpu.VMEM((GROUPS, own, 3, dh, 2 * fwh), BF),
            pltpu.VMEM((own, 3, dh, fwh), F32),
            pltpu.VMEM((own, 3, dh, fwh), F32),
            pltpu.VMEM((own, 3, dh, fwh), F32),
            pltpu.VMEM((2, 2, fwh, rows), F32),
            pltpu.VMEM((2, fwh, rows), BF),
            pltpu.VMEM((2 * own, 3, dh, fwh), SENT),
            pltpu.VMEM((max(mates - 1, 1), own, 3, dh, fwh), SENT),
            pltpu.VMEM((own, 3, dh, fwh), F32),
            pltpu.VMEM((own, 3, dh, fwh), SENT),
            pltpu.VMEM((own, 3, dh, fwh), SENT),
            pltpu.VMEM((own, 3, dh, fwh), BF),
            pltpu.VMEM((own, 3, dh, fwh), BF),
            pltpu.VMEM((1, rows), F32),
            pltpu.VMEM((max(nh - 1, 1), 1, rows), F32),
            pltpu.SemaphoreType.REGULAR((max(mates.bit_length(), 1),)),
            pltpu.SemaphoreType.REGULAR((max(nh.bit_length(), 1),)),
            dma((own * 3,)), dma((own * 3,)),
            dma((2 * hd,)), dma((2 * hd,)),
            dma((own,)), dma((own,)),
            dma((own,)), dma((own,)),
            dma((max(mates - 1, 1), own * 3)), dma((max(mates - 1, 1), own * 3)),
            dma((mates + 1, own * 3)), dma((own * 3,)),
            dma((own * 3,)), dma((own * 3,)),
            dma((max(nh - 1, 1),)), dma((max(nh - 1, 1),)),
        ],
        compiler_params=pltpu.CompilerParams(
            collective_id=0, has_side_effects=True, vmem_limit_bytes=56 * 1024 * 1024
        ),
    )(
        queries, key_rows, values, gate_init, up_init, down_init, step_size, head_scale,
    )
    return (scaled * out_gain[None, :]).astype(BF)


def solution(mesh):
    in_specs = (
        P("frame", "head"),
        P("frame", "head"),
        P("frame", "head"),
        P("head", None, None),
        P("head", None, None),
        P("head", None, None),
        P("head"),
        P("head"),
        P("head"),
    )
    return jax.shard_map(
        shards, mesh=mesh, in_specs=in_specs, out_specs=P("frame", "head"), check_vma=False
    )
```

time: 38.1 us -> 32 us (0.84)
  the two profiles are of different devices: /device:TPU:25 before, /device:TPU:17 now
where the time goes in v1:
time: 32 us; the launch traced here: 31.9 us
  Pallas kernels  31.1 us (97%)
  other arithmetic  0.74 us (2%)
    pallas_call x1, Pallas kernels, shards(): pl.pallas_call(functools.partial(kernel, (frames, nh, hd)), out_shape=plt...  31.1 us
    convert_element_type x1, other arithmetic, shards(): return (scaled * out_gain[None, :]).astype(BF)  0.74 us

profile of v1, /device:TPU:17, one launch (start us, length us, event | category | flops | bytes accessed | tf_op | source)
XLA Modules:
  0.0 31.9 jit_solution(3156556514854843749)
XLA Ops:
  0.0 0.0 copy-start
  0.0 31.1 %shard_map.91 = f32[512,256]{1,0:T(8,128)S(1)} custom-call(bf16[512,256]{1,0:T(8,128)(2,1)} %q_any.1, bf16[512,256]{1,0:T(8,128)(2,1)} %k_any.1, bf16[512,256]{1,0:T(8,128)(2,1)} %v_any.1, f32[2,128,128]{2,1,0:T(8,128)} %gate_any.1, f32[2,128,128]{2,1,0:T(8,128)} %up_any.1, f32[2,128,128]{2,1,0:T(8,128)} %down_any.1, f32[2]{0:T(128)} %step_any.1, f32[2]{0:T(128)} %scale_any.1), custom_call_target="tpu_custom_call" | custom-call | tf_op jit(solution)/shard_map/pallas_call | solution.py:657
  31.1 0.0 copy-done
  31.2 0.7 %multiply_convert_fusion = bf16[512,256]{1,0:T(8,128)(2,1)} fusion(f32[512,256]{1,0:T(8,128)S(1)} %shard_map.91, f32[256]{0:T(256)S(1)} %copy-done), kind=kLoop, calls=%fused_computation | loop fusion | flops 262144 | bytes 787456 | tf_op jit(solution)/shard_map/convert_element_type | solution.py:713
Async XLA Ops:
  0.0 31.1 %copy-start = (f32[256]{0:T(256)S(1)}, f32[256]{0:T(256)}, u32[]{:S(2)}) copy-start(f32[256]{0:T(256)} %param.17) | copy-start | bytes 3076

commit v2 on v1

--- a/solution.py
+++ b/solution.py
@@ -93,7 +93,7 @@
     q_any, k_any, v_any, gate_any, up_any, down_any, step_any, scale_any,
     out_ref,
     qs, ks, vs, gate_ref, up_ref, down_ref, step_ref, scale_ref, local_sem,
-    kp, here, before, mix, top, den, att, qn, comb, wb, wf, target, gp, hid, backs, cs, rz, tot, fw, by, wo, wr, part, others, frame_sem, head_sem, by_send, by_recv,
+    kp, here, before, mix, top, den, att, qn, comb, wb, wf, target, gp, hid, backs, cs, rz, tot, fw, wo, wr, part, others, frame_sem, head_sem,
     kv_send, kv_recv, y_send, y_recv, att_send, att_recv, mate_send, mate_recv, fw_send, fw_recv,
     w_send, w_recv, head_send, head_recv,
 ):
@@ -237,8 +237,8 @@
 
     @pl.when(has_next)
     def _():
-        for n in range(hd):
-            for which in range(2):
+        for which in range(2):
+            for n in range(hd):
                 kv_copy(n, which).start()
 
     @pl.when(core == 1)
@@ -315,8 +315,9 @@
         mean = jnp.mean(m * m, axis=1, keepdims=True)
         att[n] = (m * lax.rsqrt(mean + 1e-06)).astype(BF)
 
+    for n in range(hd):
+        weigh(n)
     for n in range(own):
-        weigh(n)
         attend(n)
         att_copy(n).start()
     rounds()
@@ -349,27 +350,19 @@
     def relay(i, m):
         return fw_copy(fw.at[i, m], beyond, 0, i, m)
 
-    def aside(i, m):
-        return pltpu.make_async_remote_copy(
-            src_ref=cs.at[own + i, m],
-            dst_ref=by.at[i, m],
-            send_sem=by_send.at[i * 3 + m],
-            recv_sem=by_recv.at[i * 3 + m],
-            device_id=(pair, j),
-            device_id_type=MESH,
-        )
-
-    def behalf(i, m):
-        return fw_copy(by.at[i, m], ahead, mates, i, m)
-
-    def fw_sends(c, i, m):
-        if m == ORDER[-1]:
-            return [fw_direct(k, i, m) for k in reversed(range(mates))]
-        if c == 1:
-            return [fw_direct(0, i, m)]
-        return [fw_direct(k, i, m) for k in reversed(range(1, mates))] + [aside(i, m)]
-
-    relays = jnp.logical_and(core == 1, p < frames - 2)
+    def fw_sends(c, m):
+        near = [(0, i, m) for i in range(own)]
+        if c == 1 or m == ORDER[0]:
+            return near
+        far = [(k, i, m) for i in range(own) for k in reversed(range(1, mates))]
+        if m != ORDER[-1]:
+            return far
+        return far + [(0, i, ORDER[1]) for i in range(own)] + near
+
+    def relayed(c):
+        return ORDER if c == 1 else ORDER[:1]
+
+    relays = [jnp.logical_and(core == c, p < frames - 2) for c in range(2)]
     closes = jnp.logical_and(seg == 0, is_last)
 
     def w_copy(i, m):
@@ -453,11 +446,12 @@
             tot[i, m] = total
             cs[own + i, m] = total.astype(SENT)
 
-        for c in range(2):
-            @pl.when(jnp.logical_and(is_last, core == c))
-            def _(c=c):
-                for copy in fw_sends(c, i, m):
-                    copy.start()
+        if i == own - 1:
+            for c in range(2):
+                @pl.when(jnp.logical_and(is_last, core == c))
+                def _(c=c):
+                    for at in fw_sends(c, m):
+                        fw_direct(*at).start()
 
     def pair_wait(i):
         att_copy(i).wait_recv()
@@ -488,7 +482,6 @@
             fast_grads(0, i, [early_set(i)], keep)
 
     for n in range(own, hd):
-        weigh(n)
         attend(n)
 
     @pl.when(jnp.logical_and(opening, jnp.logical_not(prev_far)))
@@ -507,13 +500,6 @@
                     pair_wait(i)
                     fast_grads(s, i, [(own + i, own + i), pair_set(i)], share)
             if s == 0:
-                @pl.when(jnp.logical_and(is_last, core == 1))
-                def _():
-                    for m in ORDER[:-1]:
-                        for i in range(own):
-                            aside(i, m).wait_recv()
-                            behalf(i, m).start()
-
                 @pl.when(is_last)
                 def _():
                     for m in ORDER:
@@ -536,10 +522,11 @@
                 for m in ORDER:
                     for i in range(own):
                         relay(i, m).wait_recv()
-                        if m != ORDER[-1]:
-                            @pl.when(relays)
-                            def _(i=i, m=m):
-                                relay(i, m).start()
+                        for c in range(2):
+                            if m in relayed(c):
+                                @pl.when(relays[c])
+                                def _(i=i, m=m):
+                                    relay(i, m).start()
 
                         tot[i, m] = fw[i, m].astype(F32)
 
@@ -630,18 +617,15 @@
     for c in range(2):
         @pl.when(jnp.logical_and(closes, core == c))
         def _(c=c):
+            for m in ORDER:
+                for at in fw_sends(c, m):
+                    fw_direct(*at).wait_send()
+
+        @pl.when(jnp.logical_and(seg > 0, relays[c]))
+        def _(c=c):
             for i in range(own):
-                for m in range(3):
-                    for copy in fw_sends(c, i, m):
-                        copy.wait_send()
-                    if c == 1 and m != ORDER[-1]:
-                        behalf(i, m).wait_send()
-
-    @pl.when(jnp.logical_and(seg > 0, relays))
-    def _():
-        for i in range(own):
-            for m in ORDER[:-1]:
-                relay(i, m).wait_send()
+                for m in relayed(c):
+                    relay(i, m).wait_send()
 
 
 def shards(
@@ -688,19 +672,17 @@
             pltpu.VMEM((max(mates - 1, 1), own, 3, dh, fwh), SENT),
             pltpu.VMEM((own, 3, dh, fwh), F32),
             pltpu.VMEM((own, 3, dh, fwh), SENT),
-            pltpu.VMEM((own, 3, dh, fwh), SENT),
             pltpu.VMEM((own, 3, dh, fwh), BF),
             pltpu.VMEM((own, 3, dh, fwh), BF),
             pltpu.VMEM((1, rows), F32),
             pltpu.VMEM((max(nh - 1, 1), 1, rows), F32),
             pltpu.SemaphoreType.REGULAR((max(mates.bit_length(), 1),)),
             pltpu.SemaphoreType.REGULAR((max(nh.bit_length(), 1),)),
-            dma((own * 3,)), dma((own * 3,)),
             dma((2 * hd,)), dma((2 * hd,)),
             dma((own,)), dma((own,)),
             dma((own,)), dma((own,)),
             dma((max(mates - 1, 1), own * 3)), dma((max(mates - 1, 1), own * 3)),
-            dma((mates + 1, own * 3)), dma((own * 3,)),
+            dma((mates, own * 3)), dma((own * 3,)),
             dma((own * 3,)), dma((own * 3,)),
             dma((max(nh - 1, 1),)), dma((max(nh - 1, 1),)),
         ],

time: 32 us -> 31.9 us (level)
  no operation moved by 1% of the time
where the time goes in v2:
time: 31.9 us; the launch traced here: 31.7 us
  Pallas kernels  30.9 us (97%)
  other arithmetic  0.74 us (2%)
    pallas_call x1, Pallas kernels, shards(): pl.pallas_call(functools.partial(kernel, (frames, nh, hd)), out_shape=plt...  30.9 us
    convert_element_type x1, other arithmetic, shards(): return (scaled * out_gain[None, :]).astype(BF)  0.74 us

profile of v2, /device:TPU:17, one launch (start us, length us, event | category | flops | bytes accessed | tf_op | source)
XLA Modules:
  0.0 31.7 jit_solution(7282318056521739295)
XLA Ops:
  0.0 0.0 copy-start
  0.0 30.9 %shard_map.91 = f32[512,256]{1,0:T(8,128)S(1)} custom-call(bf16[512,256]{1,0:T(8,128)(2,1)} %q_any.1, bf16[512,256]{1,0:T(8,128)(2,1)} %k_any.1, bf16[512,256]{1,0:T(8,128)(2,1)} %v_any.1, f32[2,128,128]{2,1,0:T(8,128)} %gate_any.1, f32[2,128,128]{2,1,0:T(8,128)} %up_any.1, f32[2,128,128]{2,1,0:T(8,128)} %down_any.1, f32[2]{0:T(128)} %step_any.1, f32[2]{0:T(128)} %scale_any.1), custom_call_target="tpu_custom_call" | custom-call | tf_op jit(solution)/shard_map/pallas_call | solution.py:641
  31.0 0.0 copy-done
  31.0 0.7 %multiply_convert_fusion = bf16[512,256]{1,0:T(8,128)(2,1)} fusion(f32[512,256]{1,0:T(8,128)S(1)} %shard_map.91, f32[256]{0:T(256)S(1)} %copy-done), kind=kLoop, calls=%fused_computation | loop fusion | flops 262144 | bytes 787456 | tf_op jit(solution)/shard_map/convert_element_type | solution.py:695
Async XLA Ops:
  0.0 31.0 %copy-start = (f32[256]{0:T(256)S(1)}, f32[256]{0:T(256)}, u32[]{:S(2)}) copy-start(f32[256]{0:T(256)} %param.17) | copy-start | bytes 3076

commit v3 on v1

--- a/solution.py
+++ b/solution.py
@@ -92,7 +92,7 @@
     dims,
     q_any, k_any, v_any, gate_any, up_any, down_any, step_any, scale_any,
     out_ref,
-    qs, ks, vs, gate_ref, up_ref, down_ref, step_ref, scale_ref, local_sem,
+    qs, ks, vs, w_ref, step_ref, scale_ref, local_sem,
     kp, here, before, mix, top, den, att, qn, comb, wb, wf, target, gp, hid, backs, cs, rz, tot, fw, by, wo, wr, part, others, frame_sem, head_sem, by_send, by_recv,
     kv_send, kv_recv, y_send, y_recv, att_send, att_recv, mate_send, mate_recv, fw_send, fw_recv,
     w_send, w_recv, head_send, head_recv,
@@ -121,16 +121,18 @@
         return pl.ds(pl.multiple_of(h * dh, dh), dh)
 
     mine = pl.ds(core * own, own)
-    moves = []
-    for n in range(hd):
-        cols = cols_of(head_of(n, core))
-        for src, dst in ((k_any, ks), (q_any, qs), (v_any, vs)):
-            moves.append((src.at[:, cols], dst.at[n]))
-    moves += [
-        (gate_any.at[mine], gate_ref), (up_any.at[mine], up_ref), (down_any.at[mine], down_ref),
-        (step_any, step_ref), (scale_any, scale_ref),
-    ]
-    locals_ = [pltpu.make_async_copy(src, dst, local_sem.at[n]) for n, (src, dst) in enumerate(moves)]
+    locals_ = []
+    for at, (src, dst) in enumerate(((k_any, ks), (q_any, qs), (v_any, vs))):
+        for n in range(hd):
+            cols = cols_of(head_of(n, core))
+            locals_.append(pltpu.make_async_copy(src.at[:, cols], dst.at[n], local_sem.at[at]))
+    for m, src in enumerate((gate_any, up_any, down_any)):
+        locals_.append(pltpu.make_async_copy(src.at[mine], w_ref.at[m], local_sem.at[3]))
+    locals_.append(pltpu.make_async_copy(step_any, step_ref, local_sem.at[4]))
+    locals_.append(pltpu.make_async_copy(scale_any, scale_ref, local_sem.at[5]))
+
+    def settle(ref, sem):
+        pltpu.make_async_copy(ref, ref, sem).wait()
 
     barrier = pltpu.get_barrier_semaphore()
 
@@ -209,7 +211,7 @@
         return pltpu.make_async_remote_copy(
             src_ref=src.at[:, cols],
             dst_ref=dst,
-            send_sem=kv_send.at[2 * n + which],
+            send_sem=kv_send,
             recv_sem=kv_recv.at[2 * n + which],
             device_id=(ahead, j),
             device_id_type=MESH,
@@ -237,8 +239,8 @@
 
     @pl.when(has_next)
     def _():
-        for n in range(hd):
-            for which in range(2):
+        for which in range(2):
+            for n in range(hd):
                 kv_copy(n, which).start()
 
     @pl.when(core == 1)
@@ -255,7 +257,11 @@
 
     block = min(rows, 256)
 
-    for copy in locals_:
+    settle(ks, local_sem.at[0])
+    settle(qs, local_sem.at[1])
+    settle(vs.at[pl.ds(0, hd)], local_sem.at[2])
+    settle(w_ref, local_sem.at[3])
+    for copy in locals_[-2:]:
         copy.wait()
 
     def exps(q, keys):
@@ -275,8 +281,8 @@
         mean = jnp.mean(qf * qf, axis=1, keepdims=True)
         qn[n] = (qf * lax.rsqrt(mean + 1e-06)).astype(BF)
     for i in range(own):
-        for m, ref in enumerate((gate_ref, up_ref, down_ref)):
-            w = ref[i]
+        for m in range(3):
+            w = w_ref[m, i]
             w = w.T if AXES[m] else w
             wf[i, m] = w
             target[i, m] = jnp.broadcast_to(lengths(w, AXES[m]), w.shape)
@@ -315,8 +321,9 @@
         mean = jnp.mean(m * m, axis=1, keepdims=True)
         att[n] = (m * lax.rsqrt(mean + 1e-06)).astype(BF)
 
+    for n in range(hd):
+        weigh(n)
     for n in range(own):
-        weigh(n)
         attend(n)
         att_copy(n).start()
     rounds()
@@ -325,7 +332,7 @@
         return pltpu.make_async_remote_copy(
             src_ref=cs.at[i, m],
             dst_ref=rz.at[step - 1, i, m],
-            send_sem=mate_send.at[step - 1, i * 3 + m],
+            send_sem=mate_send.at[step - 1],
             recv_sem=mate_recv.at[step - 1, i * 3 + m],
             device_id=(mate_at(step), j),
             device_id_type=MESH,
@@ -337,7 +344,7 @@
         return pltpu.make_async_remote_copy(
             src_ref=src,
             dst_ref=fw.at[i, m],
-            send_sem=fw_send.at[k, i * 3 + m],
+            send_sem=fw_send.at[k],
             recv_sem=fw_recv.at[i * 3 + m],
             device_id=(frame_at, j),
             device_id_type=MESH,
@@ -353,21 +360,24 @@
         return pltpu.make_async_remote_copy(
             src_ref=cs.at[own + i, m],
             dst_ref=by.at[i, m],
-            send_sem=by_send.at[i * 3 + m],
+            send_sem=by_send,
             recv_sem=by_recv.at[i * 3 + m],
             device_id=(pair, j),
             device_id_type=MESH,
         )
 
-    def behalf(i, m):
-        return fw_copy(by.at[i, m], ahead, mates, i, m)
+    def behalf(k, i, m):
+        return fw_copy(by.at[i, m], half + 2 * k, k, i, m)
+
+    fars = list(reversed(range(1, mates)))
 
     def fw_sends(c, i, m):
+        near = [fw_direct(0, i, m)]
+        if c == 1:
+            return near
         if m == ORDER[-1]:
-            return [fw_direct(k, i, m) for k in reversed(range(mates))]
-        if c == 1:
-            return [fw_direct(0, i, m)]
-        return [fw_direct(k, i, m) for k in reversed(range(1, mates))] + [aside(i, m)]
+            return [fw_direct(k, i, m) for k in fars] + near
+        return near + [aside(i, m)]
 
     relays = jnp.logical_and(core == 1, p < frames - 2)
     closes = jnp.logical_and(seg == 0, is_last)
@@ -376,8 +386,8 @@
         return pltpu.make_async_remote_copy(
             src_ref=wo.at[i, m],
             dst_ref=wr.at[i, m],
-            send_sem=w_send.at[i * 3 + m],
-            recv_sem=w_recv.at[i * 3 + m],
+            send_sem=w_send,
+            recv_sem=w_recv,
             device_id=(pair, j),
             device_id_type=MESH,
         )
@@ -488,7 +498,6 @@
             fast_grads(0, i, [early_set(i)], keep)
 
     for n in range(own, hd):
-        weigh(n)
         attend(n)
 
     @pl.when(jnp.logical_and(opening, jnp.logical_not(prev_far)))
@@ -512,7 +521,8 @@
                     for m in ORDER[:-1]:
                         for i in range(own):
                             aside(i, m).wait_recv()
-                            behalf(i, m).start()
+                            for k in fars:
+                                behalf(k, i, m).start()
 
                 @pl.when(is_last)
                 def _():
@@ -536,10 +546,10 @@
                 for m in ORDER:
                     for i in range(own):
                         relay(i, m).wait_recv()
-                        if m != ORDER[-1]:
-                            @pl.when(relays)
-                            def _(i=i, m=m):
-                                relay(i, m).start()
+
+                        @pl.when(relays)
+                        def _(i=i, m=m):
+                            relay(i, m).start()
 
                         tot[i, m] = fw[i, m].astype(F32)
 
@@ -566,9 +576,8 @@
     ones = jnp.ones((8, dh), BF)
     sums = jnp.zeros((8, rows), F32)
     for n in [*range(own, hd), *range(own)]:
-        if n < own:
-            for m in range(3):
-                w_copy(n, m).wait_recv()
+        if n == 0:
+            settle(wr, w_recv)
         final = wr if n < own else wo
         i = n if n < own else n - own
         x = qn[n]
@@ -588,8 +597,8 @@
         return pltpu.make_async_remote_copy(
             src_ref=part,
             dst_ref=others.at[step - 1],
-            send_sem=head_send.at[step - 1],
-            recv_sem=head_recv.at[step - 1],
+            send_sem=head_send,
+            recv_sem=head_recv,
             device_id=(p, head_at(step)),
             device_id_type=MESH,
         )
@@ -597,8 +606,9 @@
     for step in range(1, nh):
         head_copy(step).start()
     total = sums[:1]
+    if nh > 1:
+        settle(others, head_recv)
     for step in range(1, nh):
-        head_copy(step).wait_recv()
         total = total + others[step - 1]
     total = jnp.broadcast_to(total, (8, rows))
     high, low = split(lax.rsqrt(total / (width * nh) + 1e-05))
@@ -607,14 +617,12 @@
     for n in range(hd):
         out_ref[:, cols_of(head_of(n, core))] = comb[n] * inverse
 
-    for step in range(1, nh):
-        head_copy(step).wait_send()
+    if nh > 1:
+        settle(others, head_send)
 
     @pl.when(has_next)
     def _():
-        for n in range(hd):
-            for which in range(2):
-                kv_copy(n, which).wait_send()
+        settle(vs.at[pl.ds(0, 2 * hd)], kv_send)
 
     @pl.when(core == 1)
     def _():
@@ -623,25 +631,21 @@
 
     for i in range(own):
         att_copy(i).wait_send()
-        for m in range(3):
-            w_copy(i, m).wait_send()
-            for step in range(1, mates):
-                mate_copy(step, i, m).wait_send()
+    settle(wo, w_send)
+    for step in range(1, mates):
+        settle(cs.at[pl.ds(0, own)], mate_send.at[step - 1])
     for c in range(2):
         @pl.when(jnp.logical_and(closes, core == c))
         def _(c=c):
-            for i in range(own):
-                for m in range(3):
-                    for copy in fw_sends(c, i, m):
-                        copy.wait_send()
-                    if c == 1 and m != ORDER[-1]:
-                        behalf(i, m).wait_send()
+            settle(fw, fw_send.at[0])
+            for k in fars:
+                settle(fw.at[:, pl.ds(0, 1 + c)], fw_send.at[k])
+            if c == 0:
+                settle(fw.at[:, pl.ds(0, 2)], by_send)
 
     @pl.when(jnp.logical_and(seg > 0, relays))
     def _():
-        for i in range(own):
-            for m in ORDER[:-1]:
-                relay(i, m).wait_send()
+        settle(fw, fw_send.at[0])
 
 
 def shards(
@@ -663,12 +667,10 @@
             pltpu.VMEM((hd, rows, dh), BF),
             pltpu.VMEM((hd, rows, dh), BF),
             pltpu.VMEM((2 * hd + own, rows, dh), BF),
-            pltpu.VMEM((own, dh, fwh), F32),
-            pltpu.VMEM((own, dh, fwh), F32),
-            pltpu.VMEM((own, fwh, dh), F32),
+            pltpu.VMEM((3, own, dh, fwh), F32),
             pltpu.SMEM((hd,), F32),
             pltpu.SMEM((hd,), F32),
-            dma((3 * hd + 5,)),
+            dma((6,)),
             pltpu.VMEM((hd, rows, dh), BF),
             pltpu.VMEM((hd, rows, rows), F32),
             pltpu.VMEM((hd, rows, rows), BF),
@@ -693,16 +695,16 @@
             pltpu.VMEM((own, 3, dh, fwh), BF),
             pltpu.VMEM((1, rows), F32),
             pltpu.VMEM((max(nh - 1, 1), 1, rows), F32),
-            pltpu.SemaphoreType.REGULAR((max(mates.bit_length(), 1),)),
-            pltpu.SemaphoreType.REGULAR((max(nh.bit_length(), 1),)),
-            dma((own * 3,)), dma((own * 3,)),
-            dma((2 * hd,)), dma((2 * hd,)),
+            pltpu.SemaphoreType.REGULAR((max((mates - 1).bit_length(), 1),)),
+            pltpu.SemaphoreType.REGULAR((max(nh.bit_length() - 2, 1),)),
+            dma(()), dma((own * 3,)),
+            dma(()), dma((2 * hd,)),
             dma((own,)), dma((own,)),
             dma((own,)), dma((own,)),
-            dma((max(mates - 1, 1), own * 3)), dma((max(mates - 1, 1), own * 3)),
-            dma((mates + 1, own * 3)), dma((own * 3,)),
-            dma((own * 3,)), dma((own * 3,)),
-            dma((max(nh - 1, 1),)), dma((max(nh - 1, 1),)),
+            dma((max(mates - 1, 1),)), dma((max(mates - 1, 1), own * 3)),
+            dma((mates,)), dma((own * 3,)),
+            dma(()), dma(()),
+            dma(()), dma(()),
         ],
         compiler_params=pltpu.CompilerParams(
             collective_id=0, has_side_effects=True, vmem_limit_bytes=56 * 1024 * 1024

time: 32 us -> 31.4 us (0.981)
  Pallas kernels: 31.1 us -> 30.4 us
    pallas_call x1, Pallas kernels: 31.1 us -> 30.4 us  [shards(): pl.pallas_call(functools.partial(kernel, (frames, nh, hd)), out_shape=plt...]
where the time goes in v3:
time: 31.4 us; the launch traced here: 31.2 us
  Pallas kernels  30.4 us (97%)
  other arithmetic  0.74 us (2%)
    pallas_call x1, Pallas kernels, shards(): pl.pallas_call(functools.partial(kernel, (frames, nh, hd)), out_shape=plt...  30.4 us
    convert_element_type x1, other arithmetic, shards(): return (scaled * out_gain[None, :]).astype(BF)  0.74 us

profile of v3, /device:TPU:17, one launch (start us, length us, event | category | flops | bytes accessed | tf_op | source)
XLA Modules:
  0.0 31.2 jit_solution(6804051676523887809)
XLA Ops:
  0.0 0.0 copy-start
  0.0 30.4 %shard_map.91 = f32[512,256]{1,0:T(8,128)S(1)} custom-call(bf16[512,256]{1,0:T(8,128)(2,1)} %q_any.1, bf16[512,256]{1,0:T(8,128)(2,1)} %k_any.1, bf16[512,256]{1,0:T(8,128)(2,1)} %v_any.1, f32[2,128,128]{2,1,0:T(8,128)} %gate_any.1, f32[2,128,128]{2,1,0:T(8,128)} %up_any.1, f32[2,128,128]{2,1,0:T(8,128)} %down_any.1, f32[2]{0:T(128)} %step_any.1, f32[2]{0:T(128)} %scale_any.1), custom_call_target="tpu_custom_call" | custom-call | tf_op jit(solution)/shard_map/pallas_call | solution.py:661
  30.4 0.0 copy-done
  30.4 0.7 %multiply_convert_fusion = bf16[512,256]{1,0:T(8,128)(2,1)} fusion(f32[512,256]{1,0:T(8,128)S(1)} %shard_map.91, f32[256]{0:T(256)S(1)} %copy-done), kind=kLoop, calls=%fused_computation | loop fusion | flops 262144 | bytes 787456 | tf_op jit(solution)/shard_map/convert_element_type | solution.py:715
Async XLA Ops:
  0.0 30.4 %copy-start = (f32[256]{0:T(256)S(1)}, f32[256]{0:T(256)}, u32[]{:S(2)}) copy-start(f32[256]{0:T(256)} %param.17) | copy-start | bytes 3076

commit v4 on v3

--- a/solution.py
+++ b/solution.py
@@ -62,14 +62,16 @@
 
 
 def newton_schulz(grads):
-    xs = []
-    for m in grads:
-        norm = jnp.sqrt(jnp.sum(m * m, keepdims=True))
-        xs.append(m * (1.0 / (norm + 1e-07)))
+    scales = [1.0 / (jnp.sqrt(jnp.sum(m * m, keepdims=True)) + 1e-07) for m in grads]
+    xs = [m * r for m, r in zip(grads, scales)]
     for step in range(NS_ITERS):
         fine = step >= COARSE
         halves = [parts_of(x, fine) for x in xs]
-        squares = [dot_nt(left(h), right(h, 1)) for h in halves]
+        if step == 0 and not fine:
+            raw = [m.astype(BF) for m in grads]
+            squares = [dot_nt(m, m) * (r * r) for m, r in zip(raw, scales)]
+        else:
+            squares = [dot_nt(left(h), right(h, 1)) for h in halves]
         sq = [parts_of(a, fine) for a in squares]
         quartics = [dot_nn(left(a), right(a, 0)) for a in sq]
         mixing = [quintic_terms[1] * a + quintic_terms[2] * q for a, q in zip(squares, quartics)]
@@ -93,9 +95,9 @@
     q_any, k_any, v_any, gate_any, up_any, down_any, step_any, scale_any,
     out_ref,
     qs, ks, vs, w_ref, step_ref, scale_ref, local_sem,
-    kp, here, before, mix, top, den, att, qn, comb, wb, wf, target, gp, hid, backs, cs, rz, tot, fw, by, wo, wr, part, others, frame_sem, head_sem, by_send, by_recv,
-    kv_send, kv_recv, y_send, y_recv, att_send, att_recv, mate_send, mate_recv, fw_send, fw_recv,
-    w_send, w_recv, head_send, head_recv,
+    kp, here, before, mix, top, den, att, qn, comb, wb, wf, target, gp, hid, backs, cs, rz, tot, fw, by, wo, fast, got, part, others, frame_sem, head_sem, pair_sem, out_send, qn_recv, by_send, by_recv,
+    kv_send, kv_recv, y_send, y_recv, att_recv, mate_send, mate_recv, fw_send, fw_recv,
+    fast_recv, head_send, head_recv,
 ):
     frames, nh, hd = dims
     rows, width = q_any.shape
@@ -148,6 +150,11 @@
     def flip(bit):
         return j + bit - 2 * bit * lax.rem(j // bit, 2)
 
+    def across(step):
+        if not paired:
+            return head_at(step)
+        return j + sum((bit - 2 * bit * lax.rem(j // bit, 2)) for bit in bits if step & bit)
+
     is_last = rank == mates - 1
     paired = nh & (nh - 1) == 0
     bits = [1 << k for k in range(nh.bit_length() - 1)]
@@ -227,11 +234,21 @@
             device_id_type=MESH,
         )
 
+    def qn_copy(i):
+        return pltpu.make_async_remote_copy(
+            src_ref=qn.at[i],
+            dst_ref=qn.at[hd + i],
+            send_sem=out_send,
+            recv_sem=qn_recv,
+            device_id=(pair, j),
+            device_id_type=MESH,
+        )
+
     def att_copy(i):
         return pltpu.make_async_remote_copy(
             src_ref=att.at[i],
             dst_ref=att.at[hd + i],
-            send_sem=att_send.at[i],
+            send_sem=out_send,
             recv_sem=att_recv.at[i],
             device_id=(pair, j),
             device_id_type=MESH,
@@ -281,6 +298,8 @@
         mean = jnp.mean(qf * qf, axis=1, keepdims=True)
         qn[n] = (qf * lax.rsqrt(mean + 1e-06)).astype(BF)
     for i in range(own):
+        qn_copy(i).start()
+    for i in range(own):
         for m in range(3):
             w = w_ref[m, i]
             w = w.T if AXES[m] else w
@@ -327,6 +346,7 @@
         attend(n)
         att_copy(n).start()
     rounds()
+    signal(pair_sem, pair, j)
 
     def mate_copy(step, i, m):
         return pltpu.make_async_remote_copy(
@@ -361,7 +381,7 @@
             src_ref=cs.at[own + i, m],
             dst_ref=by.at[i, m],
             send_sem=by_send,
-            recv_sem=by_recv.at[i * 3 + m],
+            recv_sem=by_recv.at[i],
             device_id=(pair, j),
             device_id_type=MESH,
         )
@@ -375,60 +395,43 @@
         near = [fw_direct(0, i, m)]
         if c == 1:
             return near
-        if m == ORDER[-1]:
-            return [fw_direct(k, i, m) for k in fars] + near
-        return near + [aside(i, m)]
+        if m == ORDER[1]:
+            return near + [aside(i, m)]
+        far = [fw_direct(k, i, m) for k in fars]
+        return near + far if m == ORDER[0] else far + near
 
     relays = jnp.logical_and(core == 1, p < frames - 2)
-    closes = jnp.logical_and(seg == 0, is_last)
-
-    def w_copy(i, m):
-        return pltpu.make_async_remote_copy(
-            src_ref=wo.at[i, m],
-            dst_ref=wr.at[i, m],
-            send_sem=w_send,
-            recv_sem=w_recv,
-            device_id=(pair, j),
-            device_id_type=MESH,
-        )
 
     always = p < frames
 
     def fast_grads(state, i, sets, finish):
+        def join(ref, at):
+            return ref[at[0]] if len(at) == 1 else over(*[ref[k] for k in at])
+
+        xs, ys = [x for x, _ in sets], [y for _, y in sets]
+        n = rows * len(sets)
+
         @pl.when(always)
         def _():
-            total = None
-            for k, (xi, yi) in enumerate(sets):
-                x = att[xi]
-                xx = side(x, x)
-                gate = dot_nt(wb[state, i, 0], xx)
-                upward = dot_nt(wb[state, i, 1], xx)
-                sig = sigmoid(gate)
-                active = gate * sig
-                hid[k, 0] = active
-                hid[k, 1] = upward * sig * (1.0 + gate * (1.0 - sig))
-                d = dot_nn((active * upward).astype(BF), vs[yi])
-                total = d if total is None else total + d
-            finish(i, 2, -total)
+            x = join(att, xs)
+            pre = dot_nt(over(wb[state, i, 0], wb[state, i, 1]), side(x, x))
+            gate, upward = pre[:dh], pre[dh:]
+            sig = sigmoid(gate)
+            active = gate * sig
+            hid[0, :, :n] = active
+            hid[1, :, :n] = upward * sig * (1.0 + gate * (1.0 - sig))
+            finish(i, 2, -dot_nn((active * upward).astype(BF), join(vs, ys)))
 
         @pl.when(always)
         def _():
-            total = None
-            for k, (xi, yi) in enumerate(sets):
-                y = vs[yi]
-                back = -dot_nt(wb[state, i, 2], side(y, y))
-                backs[k] = (back * hid[k, 0]).astype(BF)
-                d = dot_nn((back * hid[k, 1]).astype(BF), att[xi])
-                total = d if total is None else total + d
-            finish(i, 0, total)
+            y = join(vs, ys)
+            back = -dot_nt(wb[state, i, 2], side(y, y))
+            backs[:, :n] = (back * hid[0, :, :n]).astype(BF)
+            finish(i, 0, dot_nn((back * hid[1, :, :n]).astype(BF), join(att, xs)))
 
         @pl.when(always)
         def _():
-            total = None
-            for k, (xi, yi) in enumerate(sets):
-                d = dot_nn(backs[k], att[xi])
-                total = d if total is None else total + d
-            finish(i, 1, total)
+            finish(i, 1, dot_nn(backs[:, :n], join(att, xs)))
 
     def keep(i, m, value):
         gp[i, m] = value
@@ -518,11 +521,19 @@
             if s == 0:
                 @pl.when(jnp.logical_and(is_last, core == 1))
                 def _():
-                    for m in ORDER[:-1]:
-                        for i in range(own):
-                            aside(i, m).wait_recv()
-                            for k in fars:
-                                behalf(k, i, m).start()
+                    for i in range(own):
+                        aside(i, ORDER[1]).wait_recv()
+                        for k in fars:
+                            behalf(k, i, ORDER[1]).start()
+
+                for c in range(2):
+                    @pl.when(jnp.logical_and(is_last, core == c))
+                    def _(c=c):
+                        settle(fw, fw_send.at[0])
+                        for k in fars:
+                            settle(fw.at[:, pl.ds(0, 2 - c)], fw_send.at[k])
+                        if c == 0:
+                            settle(fw.at[:, pl.ds(0, 1)], by_send)
 
                 @pl.when(is_last)
                 def _():
@@ -567,49 +578,65 @@
                         wf[i, m] = w
                         wb[s + 1, i, m] = side(high, low)
 
-            @pl.when(seg == s)
-            def _():
-                for i in range(own):
-                    for m in range(3):
-                        w_copy(i, m).start()
-
-    ones = jnp.ones((8, dh), BF)
-    sums = jnp.zeros((8, rows), F32)
-    for n in [*range(own, hd), *range(own)]:
-        if n == 0:
-            settle(wr, w_recv)
-        final = wr if n < own else wo
-        i = n if n < own else n - own
-        x = qn[n]
-        gate = dot_nt(x, final[i, 0])
-        upward = dot_nt(x, final[i, 1])
-        hidden = (gate * sigmoid(gate) * upward).astype(BF)
-        out = dot_nn(hidden, final[i, 2])
-        fast = (out * scale_ref[head_of(n, core)]).astype(BF)
-        both = att[n].astype(F32) + fast.astype(F32)
-        comb[n] = both
-        high, low = split(both * both)
-        sums = sums + dot_nt(side(ones, ones), side(high, low))
-    sums = jnp.maximum(sums, 0.0)
-    part[...] = sums[:1]
-
-    def head_copy(step):
-        return pltpu.make_async_remote_copy(
-            src_ref=part,
-            dst_ref=others.at[step - 1],
+    def fast_copy(t, i):
+        return pltpu.make_async_remote_copy(
+            src_ref=fast.at[t, i],
+            dst_ref=got.at[i],
+            send_sem=out_send,
+            recv_sem=fast_recv,
+            device_id=(pair, j),
+            device_id_type=MESH,
+        )
+
+    def head_copy(t, step):
+        return pltpu.make_async_remote_copy(
+            src_ref=part.at[t],
+            dst_ref=others.at[jnp.abs(core - t) * nh + step],
             send_sem=head_send,
             recv_sem=head_recv,
-            device_id=(p, head_at(step)),
-            device_id_type=MESH,
-        )
-
-    for step in range(1, nh):
-        head_copy(step).start()
-    total = sums[:1]
-    if nh > 1:
-        settle(others, head_recv)
-    for step in range(1, nh):
-        total = total + others[step - 1]
+            device_id=(p - core + t, across(step)),
+            device_id_type=MESH,
+        )
+
+    settle(qn.at[pl.ds(0, own)], qn_recv)
+    pl.semaphore_wait(pair_sem, 1)
+    ones = jnp.ones((8, dh), BF)
+    sums = [jnp.zeros((8, rows), F32)] * 2
+    for i in range(own):
+        places = [own + i + jnp.abs(core - t) * (hd - own) for t in range(2)]
+        x = over(*[qn[at] for at in places])
+        gate = dot_nt(x, wo[i, 0])
+        upward = dot_nt(x, wo[i, 1])
+        hidden = (gate * sigmoid(gate) * upward).astype(BF)
+        out = dot_nn(hidden, wo[i, 2])
+        rounded = (out * scale_ref[core * own + i]).astype(BF)
+        for t, at in enumerate(places):
+            piece = rounded[t * rows:(t + 1) * rows]
+            fast[t, i] = piece
+            both = att[at].astype(F32) + piece.astype(F32)
+            high, low = split(both * both)
+            sums[t] = sums[t] + dot_nt(side(ones, ones), side(high, low))
+    for t in range(2):
+        part[t] = jnp.maximum(sums[t], 0.0)[:1]
+    for t in range(2):
+        for step in reversed(range(1, nh)):
+            head_copy(t, step).start()
+
+        @pl.when(core != t)
+        def _(t=t):
+            head_copy(t, 0).start()
+            for i in range(own):
+                fast_copy(t, i).start()
+
+    for i in range(own):
+        comb[own + i] = att[own + i].astype(F32) + fast[core, i].astype(F32)
+    settle(got, fast_recv)
+    for i in range(own):
+        comb[i] = att[i].astype(F32) + got[i].astype(F32)
+    settle(others.at[pl.ds(1, 2 * nh - 1)], head_recv)
+    total = part[core]
+    for at in range(1, 2 * nh):
+        total = total + others[at]
     total = jnp.broadcast_to(total, (8, rows))
     high, low = split(lax.rsqrt(total / (width * nh) + 1e-05))
     eighths = jnp.full((16, dh), 0.125, BF)
@@ -617,8 +644,7 @@
     for n in range(hd):
         out_ref[:, cols_of(head_of(n, core))] = comb[n] * inverse
 
-    if nh > 1:
-        settle(others, head_send)
+    settle(others.at[pl.ds(1, 2 * nh - 1)], head_send)
 
     @pl.when(has_next)
     def _():
@@ -629,20 +655,10 @@
         for i in range(own):
             y_copy(i).wait_send()
 
-    for i in range(own):
-        att_copy(i).wait_send()
-    settle(wo, w_send)
+    sent = pl.ds(0, 3 * own)
+    settle(vs.at[sent], out_send)
     for step in range(1, mates):
         settle(cs.at[pl.ds(0, own)], mate_send.at[step - 1])
-    for c in range(2):
-        @pl.when(jnp.logical_and(closes, core == c))
-        def _(c=c):
-            settle(fw, fw_send.at[0])
-            for k in fars:
-                settle(fw.at[:, pl.ds(0, 1 + c)], fw_send.at[k])
-            if c == 0:
-                settle(fw.at[:, pl.ds(0, 2)], by_send)
-
     @pl.when(jnp.logical_and(seg > 0, relays))
     def _():
         settle(fw, fw_send.at[0])
@@ -678,32 +694,35 @@
             pltpu.VMEM((hd, rows, 1), F32),
             pltpu.VMEM((hd, rows, 1), F32),
             pltpu.VMEM((hd + own, rows, dh), BF),
-            pltpu.VMEM((hd, rows, dh), BF),
+            pltpu.VMEM((hd + own, rows, dh), BF),
             pltpu.VMEM((hd, rows, dh), F32),
             pltpu.VMEM((GROUPS, own, 3, dh, 2 * fwh), BF),
             pltpu.VMEM((own, 3, dh, fwh), F32),
             pltpu.VMEM((own, 3, dh, fwh), F32),
             pltpu.VMEM((own, 3, dh, fwh), F32),
-            pltpu.VMEM((2, 2, fwh, rows), F32),
-            pltpu.VMEM((2, fwh, rows), BF),
+            pltpu.VMEM((2, fwh, 2 * rows), F32),
+            pltpu.VMEM((fwh, 2 * rows), BF),
             pltpu.VMEM((2 * own, 3, dh, fwh), SENT),
             pltpu.VMEM((max(mates - 1, 1), own, 3, dh, fwh), SENT),
             pltpu.VMEM((own, 3, dh, fwh), F32),
             pltpu.VMEM((own, 3, dh, fwh), SENT),
             pltpu.VMEM((own, 3, dh, fwh), SENT),
             pltpu.VMEM((own, 3, dh, fwh), BF),
-            pltpu.VMEM((own, 3, dh, fwh), BF),
-            pltpu.VMEM((1, rows), F32),
-            pltpu.VMEM((max(nh - 1, 1), 1, rows), F32),
+            pltpu.VMEM((2, own, rows, dh), BF),
+            pltpu.VMEM((own, rows, dh), BF),
+            pltpu.VMEM((2, 1, rows), F32),
+            pltpu.VMEM((2 * nh, 1, rows), F32),
             pltpu.SemaphoreType.REGULAR((max((mates - 1).bit_length(), 1),)),
             pltpu.SemaphoreType.REGULAR((max(nh.bit_length() - 2, 1),)),
-            dma(()), dma((own * 3,)),
+            pltpu.SemaphoreType.REGULAR,
+            dma(()), dma(()),
+            dma(()), dma((own,)),
             dma(()), dma((2 * hd,)),
             dma((own,)), dma((own,)),
-            dma((own,)), dma((own,)),
+            dma((own,)),
             dma((max(mates - 1, 1),)), dma((max(mates - 1, 1), own * 3)),
             dma((mates,)), dma((own * 3,)),
-            dma(()), dma(()),
+            dma(()),
             dma(()), dma(()),
         ],
         compiler_params=pltpu.CompilerParams(

time: 31.4 us -> 30.6 us (0.975)
  Pallas kernels: 30.4 us -> 29.7 us
    pallas_call x1, Pallas kernels: 30.4 us -> 29.7 us  [shards(): pl.pallas_call(functools.partial(kernel, (frames, nh, hd)), out_shape=plt...]
where the time goes in v4:
time: 30.6 us; the launch traced here: 30.4 us
  Pallas kernels  29.7 us (97%)
  other arithmetic  0.74 us (2%)
    pallas_call x1, Pallas kernels, shards(): pl.pallas_call(functools.partial(kernel, (frames, nh, hd)), out_shape=plt...  29.7 us
    convert_element_type x1, other arithmetic, shards(): return (scaled * out_gain[None, :]).astype(BF)  0.74 us

profile of v4, /device:TPU:17, one launch (start us, length us, event | category | flops | bytes accessed | tf_op | source)
XLA Modules:
  0.0 30.4 jit_solution(18236760582192552361)
XLA Ops:
  0.0 0.0 copy-start
  0.0 29.7 %shard_map.91 = f32[512,256]{1,0:T(8,128)S(1)} custom-call(bf16[512,256]{1,0:T(8,128)(2,1)} %q_any.1, bf16[512,256]{1,0:T(8,128)(2,1)} %k_any.1, bf16[512,256]{1,0:T(8,128)(2,1)} %v_any.1, f32[2,128,128]{2,1,0:T(8,128)} %gate_any.1, f32[2,128,128]{2,1,0:T(8,128)} %up_any.1, f32[2,128,128]{2,1,0:T(8,128)} %down_any.1, f32[2]{0:T(128)} %step_any.1, f32[2]{0:T(128)} %scale_any.1), custom_call_target="tpu_custom_call" | custom-call | tf_op jit(solution)/shard_map/pallas_call | solution.py:677
  29.7 0.0 copy-done
  29.7 0.7 %multiply_convert_fusion = bf16[512,256]{1,0:T(8,128)(2,1)} fusion(f32[512,256]{1,0:T(8,128)S(1)} %shard_map.91, f32[256]{0:T(256)S(1)} %copy-done), kind=kLoop, calls=%fused_computation | loop fusion | flops 262144 | bytes 787456 | tf_op jit(solution)/shard_map/convert_element_type | solution.py:734
Async XLA Ops:
  0.0 29.7 %copy-start = (f32[256]{0:T(256)S(1)}, f32[256]{0:T(256)}, u32[]{:S(2)}) copy-start(f32[256]{0:T(256)} %param.17) | copy-start | bytes 3076

commit v5 on v4

--- a/solution.py
+++ b/solution.py
@@ -393,11 +393,11 @@
 
     def fw_sends(c, i, m):
         near = [fw_direct(0, i, m)]
+        far = [fw_direct(k, i, m) for k in fars]
         if c == 1:
-            return near
+            return far + near if m == ORDER[-1] else near
         if m == ORDER[1]:
             return near + [aside(i, m)]
-        far = [fw_direct(k, i, m) for k in fars]
         return near + far if m == ORDER[0] else far + near
 
     relays = jnp.logical_and(core == 1, p < frames - 2)
@@ -531,7 +531,7 @@
                     def _(c=c):
                         settle(fw, fw_send.at[0])
                         for k in fars:
-                            settle(fw.at[:, pl.ds(0, 2 - c)], fw_send.at[k])
+                            settle(fw.at[:, pl.ds(0, 2)], fw_send.at[k])
                         if c == 0:
                             settle(fw.at[:, pl.ds(0, 1)], by_send)
 
@@ -558,9 +558,10 @@
                     for i in range(own):
                         relay(i, m).wait_recv()
 
-                        @pl.when(relays)
-                        def _(i=i, m=m):
-                            relay(i, m).start()
+                        if m != ORDER[-1]:
+                            @pl.when(relays)
+                            def _(i=i, m=m):
+                                relay(i, m).start()
 
                         tot[i, m] = fw[i, m].astype(F32)
 
@@ -661,7 +662,7 @@
         settle(cs.at[pl.ds(0, own)], mate_send.at[step - 1])
     @pl.when(jnp.logical_and(seg > 0, relays))
     def _():
-        settle(fw, fw_send.at[0])
+        settle(fw.at[:, pl.ds(0, 2)], fw_send.at[0])
 
 
 def shards(

time: 30.6 us -> 30.3 us (level)
  Pallas kernels: 29.7 us -> 29.3 us
    pallas_call x1, Pallas kernels: 29.7 us -> 29.3 us  [shards(): pl.pallas_call(functools.partial(kernel, (frames, nh, hd)), out_shape=plt...]
where the time goes in v5:
time: 30.3 us; the launch traced here: 30.1 us
  Pallas kernels  29.3 us (97%)
  other arithmetic  0.74 us (2%)
    pallas_call x1, Pallas kernels, shards(): pl.pallas_call(functools.partial(kernel, (frames, nh, hd)), out_shape=plt...  29.3 us
    convert_element_type x1, other arithmetic, shards(): return (scaled * out_gain[None, :]).astype(BF)  0.74 us

profile of v5, /device:TPU:17, one launch (start us, length us, event | category | flops | bytes accessed | tf_op | source)
XLA Modules:
  0.0 30.1 jit_solution(2874260453075819200)
XLA Ops:
  0.0 0.0 copy-start
  0.0 29.3 %shard_map.91 = f32[512,256]{1,0:T(8,128)S(1)} custom-call(bf16[512,256]{1,0:T(8,128)(2,1)} %q_any.1, bf16[512,256]{1,0:T(8,128)(2,1)} %k_any.1, bf16[512,256]{1,0:T(8,128)(2,1)} %v_any.1, f32[2,128,128]{2,1,0:T(8,128)} %gate_any.1, f32[2,128,128]{2,1,0:T(8,128)} %up_any.1, f32[2,128,128]{2,1,0:T(8,128)} %down_any.1, f32[2]{0:T(128)} %step_any.1, f32[2]{0:T(128)} %scale_any.1), custom_call_target="tpu_custom_call" | custom-call | tf_op jit(solution)/shard_map/pallas_call | solution.py:678
  29.4 0.0 copy-done
  29.4 0.7 %multiply_convert_fusion = bf16[512,256]{1,0:T(8,128)(2,1)} fusion(f32[512,256]{1,0:T(8,128)S(1)} %shard_map.91, f32[256]{0:T(256)S(1)} %copy-done), kind=kLoop, calls=%fused_computation | loop fusion | flops 262144 | bytes 787456 | tf_op jit(solution)/shard_map/convert_element_type | solution.py:735
Async XLA Ops:
  0.0 29.4 %copy-start = (f32[256]{0:T(256)S(1)}, f32[256]{0:T(256)}, u32[]{:S(2)}) copy-start(f32[256]{0:T(256)} %param.17) | copy-start | bytes 3076
